TPU v7x, 32 devices: a whole 2x2x4 slice. The times are simulated.
32 devices in a mesh: tm: 8 (over z, x), chan: 4 (over y, core).
Axes of the slice: x: 2, y: 2, z: 4, core: 2. Of those that a mesh axis runs over, the one named last changes fastest.
Arguments:
- samples: bfloat16 [4096, 16384], P('tm', 'chan'), may hold values from -180 to 180
- sketch: bfloat16 [16384, 512], P('chan'), may hold values from -0.046875 to 0.046875
Outputs:
- coords: float32 [4096, 512], P('tm')
- weights: float32 [4096], P('tm')
All inputs are finite; a program needn't handle non-finite values.
Results may differ from a plain program's by a relative error of at most 0.0033.
Values may be sent and summed in bfloat16 or wider, within the bound.
A program may use at most 64 MiB of HBM per device.

v0:
```python
import jax
import jax.numpy as jnp
from jax import lax
from jax.sharding import PartitionSpec as P

C = 16384
ROUNDS = 2


def shards(samples, sketch):
    sketched = lax.psum(jnp.dot(samples, sketch, preferred_element_type=jnp.float32), "chan")
    weights = jnp.ones((samples.shape[0],), jnp.float32)
    coords = jnp.zeros(sketched.shape, jnp.float32)
    for step in range(ROUNDS):
        weighted = ((weights * weights)[:, None] * sketched).astype(jnp.bfloat16)
        local_factor = jnp.einsum(
            "sc,sk->ck", samples, weighted, preferred_element_type=jnp.float32
        )
        factor = lax.psum(local_factor, "tm")
        local_gram = jnp.dot(
            factor.T, factor, precision=lax.Precision.HIGHEST, preferred_element_type=jnp.float32
        )
        gram = lax.psum(local_gram, "chan")
        lower = jnp.linalg.cholesky(gram)
        basis = lax.linalg.triangular_solve(
            lower, factor, left_side=False, lower=True, transpose_a=True
        ).astype(jnp.bfloat16)
        local_coords = jnp.dot(samples, basis, preferred_element_type=jnp.float32)
        coords = lax.psum(local_coords, "chan")
        back = jnp.einsum(
            "sk,ck->sc", coords.astype(jnp.bfloat16), basis, preferred_element_type=jnp.float32
        )
        resid = samples.astype(jnp.float32) - back
        energy = lax.psum(jnp.sum(resid * resid, axis=1), "chan")
        weights = jnp.minimum(1.0, 3.0 / jnp.sqrt(energy / C + 1e-06))
    return (coords, weights)


def solution(mesh):
    in_specs = (P("tm", "chan"), P("chan", None))
    out_specs = (P("tm", None), P("tm"))
    return jax.shard_map(shards, mesh=mesh, in_specs=in_specs, out_specs=out_specs, check_vma=False)
```

profile of v0, /device:TPU:0, one launch (start us, length us, event | category | flops | bytes accessed | tf_op | source)
XLA Modules:
  0.0 1137.1 jit_solution(4831139212829809344)
XLA Ops:
  14.0 38.9 %all-reduce.9.cloned.1.call-done = f32[512,512]{1,0:T(8,128)} async-done(((f32[512,512]{1,0:T(8,128)}), f32[512,512]{1,0:T(8,128)}) %all-reduce.9.cloned.1.call-update) | async-done | bytes 1048592 | tf_op jit(solution)/shard_map/psum | solution.py:11
  61.2 270.9 %all-reduce.11.cloned.1.call-done = f32[4096,512]{0,1:T(8,128)} async-done(((f32[4096,512]{0,1:T(8,128)}), f32[4096,512]{0,1:T(8,128)}) %all-reduce.11.cloned.1.call-update) | async-done | bytes 8388624 | tf_op jit(solution)/shard_map/psum | solution.py:19
  332.0 17.2 %fusion.87 = f32[512,512]{0,1:T(8,128)} fusion(f32[4096,512]{0,1:T(8,128)} %all-reduce.11.cloned.1.call-done), kind=kOutput, calls=%fused_computation.154 | convolution fusion | flops 12884901888 | bytes 9437184 | tf_op jit(solution)/shard_map/dot_general | solution.py:20
  349.5 35.0 %all-reduce.13.cloned.1.call-done = f32[512,512]{0,1:T(8,128)} async-done(((f32[512,512]{0,1:T(8,128)}), f32[512,512]{0,1:T(8,128)}) %all-reduce.13.cloned.1.call-update) | async-done | bytes 1048592 | tf_op jit(solution)/shard_map/psum | solution.py:23
  387.6 11.7 %cholesky.286 = f32[128,128]{1,0:T(8,128)S(1)} custom-call(f32[128,128]{1,0:T(8,128)S(1)} %cholesky.426), custom_call_target="Cholesky" | custom-call | tf_op jit(solution)/shard_map/jit(cholesky)/cholesky | solution.py:24
  399.3 9.8 custom-call.27
  410.0 11.7 %cholesky.305 = f32[128,128]{1,0:T(8,128)S(1)} custom-call(f32[128,128]{1,0:T(8,128)S(1)} %cholesky.430), custom_call_target="Cholesky" | custom-call | tf_op jit(solution)/shard_map/jit(cholesky)/cholesky | solution.py:24
  421.7 10.2 custom-call.28
  432.6 11.7 %cholesky.326 = f32[128,128]{1,0:T(8,128)S(1)} custom-call(f32[128,128]{1,0:T(8,128)S(1)} %cholesky.435), custom_call_target="Cholesky" | custom-call | tf_op jit(solution)/shard_map/jit(cholesky)/cholesky | solution.py:24
  444.9 9.8 custom-call.29
  455.4 11.7 %cholesky.343 = f32[128,128]{1,0:T(8,128)S(1)} custom-call(f32[128,128]{1,0:T(8,128)S(1)} %convolution_subtract_fusion.9), custom_call_target="Cholesky" | custom-call | tf_op jit(solution)/shard_map/jit(cholesky)/cholesky | solution.py:24
  478.9 39.3 %custom-call.30 = f32[4,128,128]{1,2,0:T(8,128)S(1)} custom-call(f32[4,128,128]{2,1,0:T(8,128)S(1)} %get-tuple-element.18), custom_call_target="InvertDiagBlocksLowerTriangular" | custom-call | tf_op jit(solution)/shard_map/triangular_solve/custom-call.3 | solution.py:25
  546.8 25.7 %all-reduce.20 = bf16[512,512]{0,1:T(8,128)(2,1)} all-reduce(f32[512,512]{0,1:T(8,128)S(1)} %convolution_bitcast_fusion.3), channel_id=1, replica_groups=mesh['tm'=8,'chan'=4] {'chan'}, use_global_device_ids=true, to_apply=%region_11.14 | all-reduce | flops 262144 | bytes 1572864 | tf_op jit(solution)/shard_map/psum | solution.py:29
  592.7 270.9 %all-reduce.15.cloned.1.call-done = f32[4096,512]{0,1:T(8,128)} async-done(((f32[4096,512]{0,1:T(8,128)}), f32[4096,512]{0,1:T(8,128)}) %all-reduce.15.cloned.1.call-update) | async-done | bytes 8388624 | tf_op jit(solution)/shard_map/psum | solution.py:19
  863.6 17.2 %fusion.88 = f32[512,512]{0,1:T(8,128)} fusion(f32[4096,512]{0,1:T(8,128)} %all-reduce.15.cloned.1.call-done), kind=kOutput, calls=%fused_computation.155 | convolution fusion | flops 12884901888 | bytes 9437184 | tf_op jit(solution)/shard_map/dot_general | solution.py:20
  881.1 35.1 %all-reduce.17.cloned.1.call-done = f32[512,512]{0,1:T(8,128)} async-done(((f32[512,512]{0,1:T(8,128)}), f32[512,512]{0,1:T(8,128)}) %all-reduce.17.cloned.1.call-update) | async-done | bytes 1048592 | tf_op jit(solution)/shard_map/psum | solution.py:23
  919.2 11.7 %cholesky.358 = f32[128,128]{1,0:T(8,128)S(1)} custom-call(f32[128,128]{1,0:T(8,128)S(1)} %cholesky.439), custom_call_target="Cholesky" | custom-call | tf_op jit(solution)/shard_map/jit(cholesky)/cholesky | solution.py:24
  931.1 9.8 custom-call.31
  941.5 11.7 %cholesky.377 = f32[128,128]{1,0:T(8,128)S(1)} custom-call(f32[128,128]{1,0:T(8,128)S(1)} %cholesky.443), custom_call_target="Cholesky" | custom-call | tf_op jit(solution)/shard_map/jit(cholesky)/cholesky | solution.py:24
  954.5 10.2 custom-call.32
  965.4 11.7 %cholesky.398 = f32[128,128]{1,0:T(8,128)S(1)} custom-call(f32[128,128]{1,0:T(8,128)S(1)} %cholesky.448), custom_call_target="Cholesky" | custom-call | tf_op jit(solution)/shard_map/jit(cholesky)/cholesky | solution.py:24
  988.2 11.7 %cholesky.415 = f32[128,128]{1,0:T(8,128)S(1)} custom-call(f32[128,128]{1,0:T(8,128)S(1)} %convolution_subtract_fusion.8), custom_call_target="Cholesky" | custom-call | tf_op jit(solution)/shard_map/jit(cholesky)/cholesky | solution.py:24
  1011.1 39.3 %custom-call.34 = f32[4,128,128]{1,2,0:T(8,128)S(1)} custom-call(f32[4,128,128]{2,1,0:T(8,128)S(1)} %get-tuple-element.19), custom_call_target="InvertDiagBlocksLowerTriangular" | custom-call | tf_op jit(solution)/shard_map/triangular_solve/custom-call.3 | solution.py:25
  1078.9 36.6 %all-reduce.19.cloned.1.call-done = f32[512,512]{0,1:T(8,128)} async-done(((f32[512,512]{0,1:T(8,128)}), f32[512,512]{0,1:T(8,128)}) %all-reduce.19.cloned.1.call-update) | async-done | bytes 1048592 | tf_op jit(solution)/shard_map/psum | solution.py:29
  (126 shorter events, 162.9 us)
Async XLA Ops:
  7.2 45.8 %all-reduce.9.cloned.1.call-start = ((), (), s32[]{:S(2)}) async-start(), calls=%async_computation | async-start | bytes 2097152 | tf_op jit(solution)/shard_map/psum | solution.py:11
  14.0 318.0 %all-reduce.11.cloned.1.call-start = ((), (), s32[]{:S(2)}) async-start(), calls=%async_computation.1 | async-start | bytes 16777216 | tf_op jit(solution)/shard_map/psum | solution.py:19
  61.1 323.5 %all-reduce.13.cloned.1.call-start = ((), (), s32[]{:S(2)}) async-start(), calls=%async_computation.2 | async-start | bytes 2097152 | tf_op jit(solution)/shard_map/psum | solution.py:23
  349.3 514.3 %all-reduce.15.cloned.1.call-start = ((), (), s32[]{:S(2)}) async-start(), calls=%async_computation.3 | async-start | bytes 16777216 | tf_op jit(solution)/shard_map/psum | solution.py:19
  527.4 16.1 %copy-start.1 = (f32[4096,128]{0,1:T(8,128)}, f32[4096,128]{0,1:T(8,128)S(1)}, u32[]{:S(2)}) copy-start(f32[4096,128]{0,1:T(8,128)S(1)} %fusion.62) | copy-start | bytes 6291460
  534.3 9.2 copy-start.5
  534.3 10.2 copy-start.2
  543.5 1.0 copy-start.7
  572.5 12.2 %copy-start.6 = (f32[512,512]{1,0:T(8,128)S(1)}, f32[512,512]{1,0:T(8,128)}, u32[]{:S(2)}) copy-start(f32[512,512]{1,0:T(8,128)} %all-reduce.9.cloned.1.call-done) | copy-start | bytes 3145732
  592.6 323.5 %all-reduce.17.cloned.1.call-start = ((), (), s32[]{:S(2)}) async-start(), calls=%async_computation.4 | async-start | bytes 2097152 | tf_op jit(solution)/shard_map/psum | solution.py:23
  880.9 234.7 %all-reduce.19.cloned.1.call-start = ((), (), s32[]{:S(2)}) async-start(), calls=%async_computation.5 | async-start | bytes 2097152 | tf_op jit(solution)/shard_map/psum | solution.py:29
  1059.5 15.9 %copy-start = (f32[4096,128]{0,1:T(8,128)}, f32[4096,128]{0,1:T(8,128)S(1)}, u32[]{:S(2)}) copy-start(f32[4096,128]{0,1:T(8,128)S(1)} %fusion.56) | copy-start | bytes 6291460
  1066.5 9.0 copy-start.4
  1066.5 9.0 copy-start.3
Sparse Core Ops, SparseCore 0:
  14.1 38.8 all-reduce.8
  61.2 270.7 all-reduce.10
  349.4 35.1 all-reduce.12
  592.8 270.8 all-reduce.14
  881.0 35.1 all-reduce.16
  1079.0 36.4 all-reduce.18
where the time goes:
time: 1140 us
  waiting for transfers between devices  688 us (60%)
  other arithmetic  241 us (21%)
  matrix products  128 us (11%)
  blocking collectives  38.2 us (3%)
  local copies, waits for them, and re-layouts  22.2 us (2%)
  between operations  19.7 us (2%)
    psum x2, waiting for transfers between devices, shards(): factor = lax.psum(local_factor, 'tm')  542 us
    another operation x29, other arithmetic, shards(): lower = jnp.linalg.cholesky(gram)  158 us
    another operation x5, other arithmetic, shards(): lax.linalg.triangular_solve(lower, factor, left_side=False, lower=True, t...  79.2 us
    psum x2, waiting for transfers between devices, shards(): gram = lax.psum(local_gram, 'chan')  70.1 us
    another operation x14, matrix products, shards(): lax.linalg.triangular_solve(lower, factor, left_side=False, lower=True, t...  50.1 us
    psum x1, waiting for transfers between devices, shards(): lax.psum(jnp.dot(samples, sketch, preferred_element_type=jnp.float32), 'c...  38.9 us
    psum x1, waiting for transfers between devices, shards(): coords = lax.psum(local_coords, 'chan')  36.6 us
    dot_general x2, matrix products, shards(): jnp.dot(factor.T, factor, precision=lax.Precision.HIGHEST, preferred_elem...  34.5 us
  transfers between devices with their start and end apart: 6, of which 6 were waited for; matrix products, arithmetic and copies ran while one was open for 0% of the time, Pallas kernels for 0%

commit v1 on v0

--- a/solution.py
+++ b/solution.py
@@ -5,6 +5,15 @@
 
 C = 16384
 ROUNDS = 2
+
+
+def added_up(x, mesh_axis):
+    size = lax.axis_size(mesh_axis)
+    total, far = (x, 1)
+    while far < size:
+        total = total + lax.ppermute(total, mesh_axis, [(i, i ^ far) for i in range(size)])
+        far = 2 * far
+    return total
 
 
 def shards(samples, sketch):
@@ -16,7 +25,7 @@
         local_factor = jnp.einsum(
             "sc,sk->ck", samples, weighted, preferred_element_type=jnp.float32
         )
-        factor = lax.psum(local_factor, "tm")
+        factor = added_up(local_factor, "tm")
         local_gram = jnp.dot(
             factor.T, factor, precision=lax.Precision.HIGHEST, preferred_element_type=jnp.float32
         )

time: 1140 us -> 2110 us (1.85)
  waiting for transfers between devices: 688 us -> 1590 us
  other arithmetic: 241 us -> 308 us
    ppermute x0 -> x6, waiting for transfers between devices: none -> 1440 us  [added_up(): lax.ppermute(total, mesh_axis, [(i, i ^ far) for i in range(size)])]
    psum x2 -> x0, waiting for transfers between devices: 542 us -> none  [shards(): factor = lax.psum(local_factor, 'tm')]
    add x0 -> x6, other arithmetic: none -> 66.8 us  [added_up(): total + lax.ppermute(total, mesh_axis, [(i, i ^ far) for i in range(size)])]
  transfers between devices with their start and end apart: 6 -> 10, of which waited for: 6 -> 10; matrix products, arithmetic and copies ran while one was open for 0% -> 0% of each run, Pallas kernels for 0% -> 0%
where the time goes in v1:
time: 2110 us; the launch traced here: 2100 us
  waiting for transfers between devices  1590 us (75%)
  other arithmetic  308 us (15%)
  matrix products  113 us (5%)
  blocking collectives  38.6 us (2%)
  local copies, waits for them, and re-layouts  28.4 us (1%)
    ppermute x6, waiting for transfers between devices, added_up(): lax.ppermute(total, mesh_axis, [(i, i ^ far) for i in range(size)])  1440 us
    another operation x29, other arithmetic, shards(): lower = jnp.linalg.cholesky(gram)  158 us
    another operation x5, other arithmetic, shards(): lax.linalg.triangular_solve(lower, factor, left_side=False, lower=True, t...  79.2 us
    psum x2, waiting for transfers between devices, shards(): gram = lax.psum(local_gram, 'chan')  73.7 us
    add x6, other arithmetic, added_up(): total + lax.ppermute(total, mesh_axis, [(i, i ^ far) for i in range(size)])  66.8 us
  transfers between devices with their start and end apart: 10, of which 10 were waited for; matrix products, arithmetic and copies ran while one was open for 0% of the time, Pallas kernels for 0%

profile of v1, /device:TPU:0, one launch (start us, length us, event | category | flops | bytes accessed | tf_op | source)
XLA Modules:
  0.0 2103.8 jit_solution(16649953715498821098)
XLA Ops:
  14.0 38.9 %all-reduce.7.cloned.1.call-done = f32[512,512]{1,0:T(8,128)} async-done(((f32[512,512]{1,0:T(8,128)}), f32[512,512]{1,0:T(8,128)}) %all-reduce.7.cloned.1.call-update) | async-done | bytes 1048592 | tf_op jit(solution)/shard_map/psum | solution.py:20
  62.6 180.6 %collective-permute-done = f32[4096,512]{0,1:T(8,128)} collective-permute-done((f32[4096,512]{0,1:T(8,128)S(1)}, f32[4096,512]{0,1:T(8,128)}, u32[]{:S(2)}, u32[]{:S(2)}) %collective-permute-start) | collective-permute-done | bytes 8388640 | tf_op jit(solution)/shard_map/ppermute | solution.py:14
  243.3 11.1 add.69
  255.6 180.1 %collective-permute-done.1 = f32[4096,512]{0,1:T(8,128)} collective-permute-done((f32[4096,512]{0,1:T(8,128)}, f32[4096,512]{0,1:T(8,128)}, u32[]{:S(2)}, u32[]{:S(2)}) %collective-permute-start.1) | collective-permute-done | bytes 8388640 | tf_op jit(solution)/shard_map/ppermute | solution.py:14
  448.8 359.2 %collective-permute-done.2 = f32[4096,512]{0,1:T(8,128)} collective-permute-done((f32[4096,512]{0,1:T(8,128)}, f32[4096,512]{0,1:T(8,128)}, u32[]{:S(2)}, u32[]{:S(2)}) %collective-permute-start.2) | collective-permute-done | bytes 8388640 | tf_op jit(solution)/shard_map/ppermute | solution.py:14
  819.2 17.2 fusion.85
  836.7 36.6 %all-reduce.9.cloned.1.call-done = f32[512,512]{0,1:T(8,128)} async-done(((f32[512,512]{0,1:T(8,128)}), f32[512,512]{0,1:T(8,128)}) %all-reduce.9.cloned.1.call-update) | async-done | bytes 1048592 | tf_op jit(solution)/shard_map/psum | solution.py:32
  876.3 11.7 cholesky.286
  898.7 11.7 cholesky.305
  921.3 11.7 cholesky.326
  944.1 11.7 cholesky.343
  967.6 39.3 %custom-call.30 = f32[4,128,128]{1,2,0:T(8,128)S(1)} custom-call(f32[4,128,128]{2,1,0:T(8,128)S(1)} %get-tuple-element.18), custom_call_target="InvertDiagBlocksLowerTriangular" | custom-call | tf_op jit(solution)/shard_map/triangular_solve/custom-call.3 | solution.py:34
  1031.0 25.7 %all-reduce.14 = bf16[512,512]{0,1:T(8,128)(2,1)} all-reduce(f32[512,512]{0,1:T(8,128)S(1)} %convolution_bitcast_fusion.3), channel_id=1, replica_groups=mesh['tm'=8,'chan'=4] {'chan'}, use_global_device_ids=true, to_apply=%region_10.13 | all-reduce | flops 262144 | bytes 1572864 | tf_op jit(solution)/shard_map/psum | solution.py:38
  1079.0 179.5 %collective-permute-done.3 = f32[4096,512]{0,1:T(8,128)} collective-permute-done((f32[4096,512]{0,1:T(8,128)S(1)}, f32[4096,512]{0,1:T(8,128)}, u32[]{:S(2)}, u32[]{:S(2)}) %collective-permute-start.3) | collective-permute-done | bytes 8388640 | tf_op jit(solution)/shard_map/ppermute | solution.py:14
  1271.2 179.1 %collective-permute-done.4 = f32[4096,512]{0,1:T(8,128)} collective-permute-done((f32[4096,512]{0,1:T(8,128)}, f32[4096,512]{0,1:T(8,128)}, u32[]{:S(2)}, u32[]{:S(2)}) %collective-permute-start.4) | collective-permute-done | bytes 8388640 | tf_op jit(solution)/shard_map/ppermute | solution.py:14
  1463.6 358.2 %collective-permute-done.5 = f32[4096,512]{0,1:T(8,128)} collective-permute-done((f32[4096,512]{0,1:T(8,128)}, f32[4096,512]{0,1:T(8,128)}, u32[]{:S(2)}, u32[]{:S(2)}) %collective-permute-start.5) | collective-permute-done | bytes 8388640 | tf_op jit(solution)/shard_map/ppermute | solution.py:14
  1832.9 17.2 fusion.86
  1850.4 37.1 %all-reduce.11.cloned.1.call-done = f32[512,512]{0,1:T(8,128)} async-done(((f32[512,512]{0,1:T(8,128)}), f32[512,512]{0,1:T(8,128)}) %all-reduce.11.cloned.1.call-update) | async-done | bytes 1048592 | tf_op jit(solution)/shard_map/psum | solution.py:32
  1890.6 11.7 cholesky.358
  1912.9 11.7 cholesky.377
  1936.8 11.7 cholesky.398
  1959.6 11.7 cholesky.415
  1982.4 39.3 %custom-call.34 = f32[4,128,128]{1,2,0:T(8,128)S(1)} custom-call(f32[4,128,128]{2,1,0:T(8,128)S(1)} %get-tuple-element.19), custom_call_target="InvertDiagBlocksLowerTriangular" | custom-call | tf_op jit(solution)/shard_map/triangular_solve/custom-call.3 | solution.py:34
  2046.9 36.6 %all-reduce.13.cloned.1.call-done = f32[512,512]{0,1:T(8,128)} async-done(((f32[512,512]{0,1:T(8,128)}), f32[512,512]{0,1:T(8,128)}) %all-reduce.13.cloned.1.call-update) | async-done | bytes 1048592 | tf_op jit(solution)/shard_map/psum | solution.py:38
  (156 shorter events, 269.9 us)
Async XLA Ops:
  7.2 45.8 %all-reduce.7.cloned.1.call-start = ((), (), s32[]{:S(2)}) async-start(), calls=%async_computation | async-start | bytes 2097152 | tf_op jit(solution)/shard_map/psum | solution.py:20
  14.0 859.3 %all-reduce.9.cloned.1.call-start = ((), (), s32[]{:S(2)}) async-start(), calls=%async_computation.1 | async-start | bytes 2097152 | tf_op jit(solution)/shard_map/psum | solution.py:32
  58.0 3.2 copy-start.1
  61.2 182.1 %collective-permute-start = (f32[4096,512]{0,1:T(8,128)S(1)}, f32[4096,512]{0,1:T(8,128)}, u32[]{:S(2)}, u32[]{:S(2)}) collective-permute-start(f32[4096,512]{0,1:T(8,128)S(1)} %convolution_bitcast_fusion.1), channel_id=1, source_target_pairs={{0,4},{4,0},{8,12},{12,8},{16,20},{20,16},{24,28},{28,24},{1,5},{5... | collective-permute-start | bytes 25165832 | tf_op jit(solution)/shard_map/ppermute | solution.py:14
  254.4 181.4 %collective-permute-start.1 = (f32[4096,512]{0,1:T(8,128)}, f32[4096,512]{0,1:T(8,128)}, u32[]{:S(2)}, u32[]{:S(2)}) collective-permute-start(f32[4096,512]{0,1:T(8,128)} %add.69), channel_id=1, source_target_pairs={{0,8},{4,12},{8,0},{12,4},{16,24},{20,28},{24,16},{28,20},{1,9},{5... | collective-permute-start | bytes 25165832 | tf_op jit(solution)/shard_map/ppermute | solution.py:14
  446.9 361.1 %collective-permute-start.2 = (f32[4096,512]{0,1:T(8,128)}, f32[4096,512]{0,1:T(8,128)}, u32[]{:S(2)}, u32[]{:S(2)}) collective-permute-start(f32[4096,512]{0,1:T(8,128)} %add.70), channel_id=1, source_target_pairs={{0,16},{4,20},{8,24},{12,28},{16,0},{20,4},{24,8},{28,12},{1,17},{... | collective-permute-start | bytes 25165832 | tf_op jit(solution)/shard_map/ppermute | solution.py:14
  836.4 1051.1 %all-reduce.11.cloned.1.call-start = ((), (), s32[]{:S(2)}) async-start(), calls=%async_computation.2 | async-start | bytes 2097152 | tf_op jit(solution)/shard_map/psum | solution.py:32
  1010.4 8.4 slice-start
  1012.4 6.4 slice-start.1
  1016.3 11.4 copy-start.3
  1020.9 6.7 copy-start.7
  1025.5 3.1 copy-start.4
  1056.6 12.7 copy-start.8
  1074.0 3.2 copy-start
  1077.2 181.3 %collective-permute-start.3 = (f32[4096,512]{0,1:T(8,128)S(1)}, f32[4096,512]{0,1:T(8,128)}, u32[]{:S(2)}, u32[]{:S(2)}) collective-permute-start(f32[4096,512]{0,1:T(8,128)S(1)} %convolution_bitcast_fusion), channel_id=1, source_target_pairs={{0,4},{4,0},{8,12},{12,8},{16,20},{20,16},{24,28},{28,24},{1,5},{5... | collective-permute-start | bytes 25165832 | tf_op jit(solution)/shard_map/ppermute | solution.py:14
  1269.7 180.6 %collective-permute-start.4 = (f32[4096,512]{0,1:T(8,128)}, f32[4096,512]{0,1:T(8,128)}, u32[]{:S(2)}, u32[]{:S(2)}) collective-permute-start(f32[4096,512]{0,1:T(8,128)} %add.73), channel_id=1, source_target_pairs={{0,8},{4,12},{8,0},{12,4},{16,24},{20,28},{24,16},{28,20},{1,9},{5... | collective-permute-start | bytes 25165832 | tf_op jit(solution)/shard_map/ppermute | solution.py:14
  1461.4 360.4 %collective-permute-start.5 = (f32[4096,512]{0,1:T(8,128)}, f32[4096,512]{0,1:T(8,128)}, u32[]{:S(2)}, u32[]{:S(2)}) collective-permute-start(f32[4096,512]{0,1:T(8,128)} %add.74), channel_id=1, source_target_pairs={{0,16},{4,20},{8,24},{12,28},{16,0},{20,4},{24,8},{28,12},{1,17},{... | collective-permute-start | bytes 25165832 | tf_op jit(solution)/shard_map/ppermute | solution.py:14
  1850.2 233.3 %all-reduce.13.cloned.1.call-start = ((), (), s32[]{:S(2)}) async-start(), calls=%async_computation.3 | async-start | bytes 2097152 | tf_op jit(solution)/shard_map/psum | solution.py:38
  2025.3 8.4 slice-start.2
  2027.3 6.4 slice-start.3
  2031.1 11.4 copy-start.2
  2035.8 6.7 copy-start.6
  2040.4 3.1 copy-start.5
  2083.4 12.3 copy-start.9
  (2 other events, 2.0 us)
Sparse Core Ops, SparseCore 0:
  14.1 38.8 all-reduce.6
  836.5 36.6 all-reduce.8
  1850.3 37.1 all-reduce.10
  2047.0 36.4 all-reduce.12
